TPU v7x, 32 devices: a whole 2x2x4 slice. The times are simulated.
32 devices in a mesh: tm: 8 (over z, x), col: 4 (over y, core).
Axes of the slice: x: 2, y: 2, z: 4, core: 2. Of those that a mesh axis runs over, the one named last changes fastest.
Arguments:
- near_prop: bfloat16 [16, 2, 512, 512], P('tm', None, None, 'col'), may hold values from -0.1875 to 0.1875
- far_prop: bfloat16 [16, 2, 512, 512], P('tm', None, None, 'col'), may hold values from -0.1875 to 0.1875
- meson: bfloat16 [16, 2, 512, 512], P('tm', None, None, 'col'), may hold values from -6 to 6
Outputs:
- blocks: float32 [16, 2, 512, 512], P('tm', None, None, 'col')
All inputs are finite; a program needn't handle non-finite values.
Results may differ from a plain program's by a relative error of at most 0.0035.
Values may be sent and summed in bfloat16 or wider, within the bound.
A program may use at most 64 MiB of HBM per device.

v0:
```python
import jax
import jax.numpy as jnp
from jax import lax
from jax.sharding import PartitionSpec as P


def from_behind(array, axis, by):
    peers = lax.axis_size(axis)
    return lax.ppermute(array, axis, [(i, (i + by) % peers) for i in range(peers)])


def complex_product(left, right):
    real_part = jnp.einsum(
        "tik,tkj->tij", left[:, 0], right[:, 0], preferred_element_type=jnp.float32
    ) - jnp.einsum("tik,tkj->tij", left[:, 1], right[:, 1], preferred_element_type=jnp.float32)
    imag_part = jnp.einsum(
        "tik,tkj->tij", left[:, 0], right[:, 1], preferred_element_type=jnp.float32
    ) + jnp.einsum("tik,tkj->tij", left[:, 1], right[:, 0], preferred_element_type=jnp.float32)
    return jnp.stack([real_part, imag_part], axis=1)


def gamma_adjoint(perambulator):
    order = perambulator.shape[2]
    signs = jnp.where(jnp.arange(order) < order // 2, 1.0, -1.0).astype(jnp.bfloat16)
    both_signs = signs[:, None] * signs[None, :]
    conjugate = jnp.stack([perambulator[:, 0], -perambulator[:, 1]], axis=1)
    return jnp.swapaxes(conjugate, 2, 3) * both_signs


def backward_block(prop_whole, meson_whole, first_column, width):
    adjoint_whole = gamma_adjoint(prop_whole)
    adjoint_cols = lax.dynamic_slice_in_dim(adjoint_whole, first_column, width, 3)
    inner = complex_product(meson_whole, adjoint_cols).astype(jnp.bfloat16)
    return complex_product(prop_whole, inner).astype(jnp.bfloat16)


def shards(near_prop, far_prop, meson):
    width = near_prop.shape[3]
    first_column = lax.axis_index("col") * width
    step_near = lax.axis_size("tm") // 8
    step_far = 3 * lax.axis_size("tm") // 8
    near_whole, far_whole, meson_whole = (
        lax.all_gather(near_prop, "col", axis=3, tiled=True),
        lax.all_gather(far_prop, "col", axis=3, tiled=True),
        lax.all_gather(meson, "col", axis=3, tiled=True),
    )
    shard_ahead_near = from_behind(meson, "tm", -step_near)
    shard_ahead_far = from_behind(meson, "tm", -step_far)
    meson_ahead_near, meson_ahead_far = (
        lax.all_gather(shard_ahead_near, "col", axis=3, tiled=True),
        lax.all_gather(shard_ahead_far, "col", axis=3, tiled=True),
    )
    ahead_near = complex_product(meson_ahead_near, near_prop).astype(jnp.bfloat16)
    total = complex_product(gamma_adjoint(near_whole), ahead_near)
    ahead_far = complex_product(meson_ahead_far, far_prop).astype(jnp.bfloat16)
    total = total + complex_product(gamma_adjoint(far_whole), ahead_far)
    local_near = backward_block(near_whole, meson_whole, first_column, width)
    local_far = backward_block(far_whole, meson_whole, first_column, width)
    arrived_near = from_behind(local_near, "tm", step_near)
    arrived_far = from_behind(local_far, "tm", step_far)
    total = total + arrived_near.astype(jnp.float32) + arrived_far.astype(jnp.float32)
    return total


def solution(mesh):
    placed = (P("tm", None, None, "col"), P("tm", None, None, "col"), P("tm", None, None, "col"))
    return jax.shard_map(
        shards, mesh=mesh, in_specs=placed, out_specs=P("tm", None, None, "col"), check_vma=False
    )
```

profile of v0, /device:TPU:29, one launch (start us, length us, event | category | flops | bytes accessed | tf_op | source)
XLA Modules:
  0.0 144.3 jit_solution(14312504081932216544)
XLA Ops:
  6.5 2.1 %copy.8 = bf16[2,2,512,128]{2,3,0,1:T(8,128)(2,1)} copy(bf16[2,2,512,128]{3,2,1,0:T(8,128)(2,1)} %param.4) | data formatting | bytes 1048576 | tf_op args[1]
  8.7 2.0 %copy.4 = bf16[2,2,512,128]{2,3,0,1:T(8,128)(2,1)} copy(bf16[2,2,512,128]{3,2,1,0:T(8,128)(2,1)} %param.3) | data formatting | bytes 1048576 | tf_op args[0]
  11.7 1.0 collective-permute-start.1
  12.8 14.7 %collective-permute-done.1 = bf16[2,2,512,128]{3,2,0,1:T(8,128)(2,1)S(1)} collective-permute-done((bf16[2,2,512,128]{3,2,0,1:T(8,128)(2,1)}, bf16[2,2,512,128]{3,2,0,1:T(8,128)(2,1)S(1)}, u32[]{:S(2)}, u32[]{:S(2)}) %collective-permute-start.1) | collective-permute-done | bytes 524320 | tf_op jit(solution)/shard_map/ppermute | solution.py:9
  28.6 0.9 broadcast_multiply_fusion
  29.6 23.4 %collective-permute-done = bf16[2,2,512,128]{3,2,0,1:T(8,128)(2,1)S(1)} collective-permute-done((bf16[2,2,512,128]{3,2,0,1:T(8,128)(2,1)}, bf16[2,2,512,128]{3,2,0,1:T(8,128)(2,1)S(1)}, u32[]{:S(2)}, u32[]{:S(2)}) %collective-permute-start) | collective-permute-done | bytes 524320 | tf_op jit(solution)/shard_map/ppermute | solution.py:9
  53.9 2.7 %fusion.80 = (bf16[2,1,512,512]{2,3,0,1:T(8,128)(2,1)S(1)}, bf16[2,1,512,512]{2,3,0,1:T(8,128)(2,1)}) fusion(bf16[2,2,512,512]{2,3,0,1:T(8,128)(2,1)} %all-gather.10.cloned.1.call-done), kind=kLoop, calls=%fused_computation.120 | loop fusion | flops 524288 | bytes 4194304 | tf_op jit(solution)/shard_map/slice | solution.py:26
  56.6 1.8 %fusion.81 = (bf16[2,1,512,512]{2,3,0,1:T(8,128)(2,1)S(1)}, bf16[2,1,512,512]{2,3,0,1:T(8,128)(2,1)S(1)}) fusion(bf16[2,2,512,512]{2,3,0,1:T(8,128)(2,1)} %all-gather.6.cloned.1.call-done), kind=kLoop, calls=%fused_computation.121 | loop fusion | flops 524288 | bytes 4194304 | tf_op jit(solution)/shard_map/slice | solution.py:26
  58.5 1.6 %fusion.1 = (bf16[2,2,512,512]{3,2,0,1:T(8,128)(2,1)}, bf16[2,2,512,512]{3,2,0,1:T(8,128)(2,1)S(1)}) fusion(bf16[2,1,512,512]{2,3,0,1:T(8,128)(2,1)S(1)} %copy-done.5, bf16[2,1,512,512]{2,3,0,1:T(8,128)(2,1)S(1)} %get-tuple-element.5, bf16[512,512]{1,0:T(8,128)(2,1)S(1)} %copy-done.6, bf16[2,1,512,512]{2,3,0,1:T(8,128)(2,1)S(1)} %get-tuple-element.8, ...), kind=kLoop, calls=%fused_computation.3 | loop fusion | flops 4194304 | bytes 8912896 | tf_op jit(solution)/shard_map/mul | solution.py:27
  60.1 20.3 %all-gather.14.cloned.1.call-done = bf16[2,2,512,512]{3,2,0,1:T(8,128)(2,1)} async-done(((bf16[2,2,512,128]{3,2,0,1:T(8,128)(2,1)}), bf16[2,2,512,512]{3,2,0,1:T(8,128)(2,1)}) %all-gather.14.cloned.1.call-update) | async-done | bytes 2097168 | tf_op jit(solution)/shard_map/all_gather | solution.py:45
  80.5 1.9 %fusion.51 = f32[2,128,512]{2,1,0:T(8,128)S(1)} fusion(bf16[2,2,512,512]{3,2,0,1:T(8,128)(2,1)} %all-gather.14.cloned.1.call-done, bf16[2,2,512,512]{3,2,0,1:T(8,128)(2,1)S(1)} %get-tuple-element.10, s32[]{:T(128)S(6)} %select_n.22), kind=kOutput, calls=%fused_computation.82 | convolution fusion | flops 134217728 | bytes 1835012 | tf_op jit(solution)/shard_map/tik,tkj->tij/dot_general | solution.py:13
  82.4 1.9 %fusion.50 = f32[2,128,512]{2,1,0:T(8,128)S(1)} fusion(bf16[2,2,512,512]{3,2,0,1:T(8,128)(2,1)} %all-gather.14.cloned.1.call-done, bf16[2,2,512,512]{3,2,0,1:T(8,128)(2,1)S(1)} %get-tuple-element.10, s32[]{:T(128)S(6)} %add.65, s32[]{:T(128)S(6)} %select_n.22), kind=kOutput, calls=%fused_computation.81 | convolution fusion | flops 134217728 | bytes 1835016 | tf_op jit(solution)/shard_map/tik,tkj->tij/dot_general | solution.py:16
  87.4 0.9 pad_maximum_fusion
  88.2 1.2 collective-permute-start.2
  93.5 0.8 pad_maximum_fusion.1
  94.4 1.1 collective-permute-start.3
  95.5 9.2 %all-gather.12.cloned.1.call-done = bf16[2,2,512,512]{3,2,0,1:T(8,128)(2,1)} async-done(((bf16[2,2,512,128]{3,2,0,1:T(8,128)(2,1)}), bf16[2,2,512,512]{3,2,0,1:T(8,128)(2,1)}) %all-gather.12.cloned.1.call-update) | async-done | bytes 2097168 | tf_op jit(solution)/shard_map/all_gather | solution.py:51
  104.7 1.8 %fusion.43 = f32[2,512,128]{2,1,0:T(8,128)S(1)} fusion(bf16[2,2,512,512]{3,2,0,1:T(8,128)(2,1)} %all-gather.12.cloned.1.call-done, bf16[2,2,512,128]{3,2,1,0:T(8,128)(2,1)S(1)} %copy-done.8), kind=kOutput, calls=%fused_computation.72 | convolution fusion | flops 134217728 | bytes 1835008 | tf_op jit(solution)/shard_map/tik,tkj->tij/dot_general | solution.py:15
  106.6 1.8 %fusion.8 = bf16[2,512,128]{2,1,0:T(8,128)(2,1)S(1)} fusion(f32[2,512,128]{2,1,0:T(8,128)S(1)} %fusion.43, bf16[2,2,512,512]{3,2,0,1:T(8,128)(2,1)} %all-gather.12.cloned.1.call-done, bf16[2,2,512,128]{3,2,1,0:T(8,128)(2,1)S(1)} %copy-done.8), kind=kOutput, calls=%fused_computation.26 | convolution fusion | flops 134479872 | bytes 2097152 | tf_op jit(solution)/shard_map/tik,tkj->tij/dot_general | solution.py:13
  111.0 17.9 %all-gather.8.cloned.1.call-done = bf16[2,2,512,512]{3,2,0,1:T(8,128)(2,1)} async-done(((bf16[2,2,512,128]{3,2,0,1:T(8,128)(2,1)}), bf16[2,2,512,512]{3,2,0,1:T(8,128)(2,1)}) %all-gather.8.cloned.1.call-update) | async-done | bytes 2097168 | tf_op jit(solution)/shard_map/all_gather | solution.py:50
  129.0 1.7 %fusion.39 = f32[2,512,128]{2,1,0:T(8,128)S(1)} fusion(bf16[2,2,512,512]{3,2,0,1:T(8,128)(2,1)} %all-gather.8.cloned.1.call-done, bf16[2,2,512,128]{3,2,1,0:T(8,128)(2,1)} %param.3), kind=kOutput, calls=%fused_computation.68 | convolution fusion | flops 134217728 | bytes 1835008 | tf_op jit(solution)/shard_map/tik,tkj->tij/dot_general | solution.py:15
  130.8 1.8 %fusion.6 = bf16[2,512,128]{2,1,0:T(8,128)(2,1)S(1)} fusion(f32[2,512,128]{2,1,0:T(8,128)S(1)} %fusion.39, bf16[2,2,512,512]{3,2,0,1:T(8,128)(2,1)} %all-gather.8.cloned.1.call-done, bf16[2,2,512,128]{3,2,1,0:T(8,128)(2,1)S(1)} %copy-done.9), kind=kOutput, calls=%fused_computation.24 | convolution fusion | flops 134479872 | bytes 2097152 | tf_op jit(solution)/shard_map/tik,tkj->tij/dot_general | solution.py:13
  135.3 1.4 fusion.23
  136.7 1.0 copy.37
  (71 shorter events, 15.6 us)
Async XLA Ops:
  6.5 4.3 %copy-start.7 = (bf16[2,2,512,128]{3,2,1,0:T(8,128)(2,1)S(1)}, bf16[2,2,512,128]{3,2,1,0:T(8,128)(2,1)}, u32[]{:S(2)}) copy-start(bf16[2,2,512,128]{3,2,1,0:T(8,128)(2,1)} %param.5) | copy-start | bytes 1572868
  6.5 47.3 %all-gather.10.cloned.1.call-start = ((), (), s32[]{:S(2)}) async-start(), calls=%async_computation.2 | async-start | bytes 2621440 | tf_op jit(solution)/shard_map/all_gather | solution.py:44
  8.7 47.9 %all-gather.6.cloned.1.call-start = ((), (), s32[]{:S(2)}) async-start(), calls=%async_computation | async-start | bytes 2621440 | tf_op jit(solution)/shard_map/all_gather | solution.py:43
  10.8 69.7 %all-gather.14.cloned.1.call-start = ((), (), s32[]{:S(2)}) async-start(), calls=%async_computation.4 | async-start | bytes 2621440 | tf_op jit(solution)/shard_map/all_gather | solution.py:45
  11.7 93.0 %all-gather.12.cloned.1.call-start = ((), (), s32[]{:S(2)}) async-start(), calls=%async_computation.3 | async-start | bytes 2621440 | tf_op jit(solution)/shard_map/all_gather | solution.py:51
  11.7 15.8 %collective-permute-start.1 = (bf16[2,2,512,128]{3,2,0,1:T(8,128)(2,1)}, bf16[2,2,512,128]{3,2,0,1:T(8,128)(2,1)S(1)}, u32[]{:S(2)}, u32[]{:S(2)}) collective-permute-start(bf16[2,2,512,128]{3,2,0,1:T(8,128)(2,1)} %copy.5), channel_id=1, source_target_pairs={{0,20},{4,24},{8,28},{12,0},{16,4},{20,8},{24,12},{28,16},{1,21},{... | collective-permute-start | bytes 1572872 | tf_op jit(solution)/shard_map/ppermute | solution.py:9
  27.5 0.8 copy-start.11
  28.3 100.7 %all-gather.8.cloned.1.call-start = ((), (), s32[]{:S(2)}) async-start(), calls=%async_computation.1 | async-start | bytes 2621440 | tf_op jit(solution)/shard_map/all_gather | solution.py:50
  28.4 24.6 %collective-permute-start = (bf16[2,2,512,128]{3,2,0,1:T(8,128)(2,1)}, bf16[2,2,512,128]{3,2,0,1:T(8,128)(2,1)S(1)}, u32[]{:S(2)}, u32[]{:S(2)}) collective-permute-start(bf16[2,2,512,128]{3,2,0,1:T(8,128)(2,1)} %copy.5), channel_id=1, source_target_pairs={{0,28},{4,0},{8,4},{12,8},{16,12},{20,16},{24,20},{28,24},{1,29},{... | collective-permute-start | bytes 1572872 | tf_op jit(solution)/shard_map/ppermute | solution.py:9
  53.0 0.8 copy-start.10
  56.6 1.9 %copy-start.5 = (bf16[2,1,512,512]{2,3,0,1:T(8,128)(2,1)S(1)}, bf16[2,1,512,512]{2,3,0,1:T(8,128)(2,1)}, u32[]{:S(2)}) copy-start(bf16[2,1,512,512]{2,3,0,1:T(8,128)(2,1)} %get-tuple-element.6) | copy-start | bytes 3145732
  56.6 2.0 %copy-start.6 = (bf16[512,512]{1,0:T(8,128)(2,1)S(1)}, bf16[512,512]{1,0:T(8,128)(2,1)}, u32[]{:S(2)}) copy-start(bf16[512,512]{1,0:T(8,128)(2,1)} %broadcast_multiply_fusion) | copy-start | bytes 1572868
  80.5 3.7 %copy-start = (bf16[2,2,512,512]{3,2,0,1:T(8,128)(2,1)S(1)}, bf16[2,2,512,512]{3,2,0,1:T(8,128)(2,1)}, u32[]{:S(2)}) copy-start(bf16[2,2,512,512]{3,2,0,1:T(8,128)(2,1)} %all-gather.14.cloned.1.call-done) | copy-start | bytes 6291460
  82.3 2.4 %copy-start.2 = (bf16[2,2,512,512]{2,3,0,1:T(8,128)(2,1)S(1)}, bf16[2,2,512,512]{2,3,0,1:T(8,128)(2,1)}, u32[]{:S(2)}) copy-start(bf16[2,2,512,512]{2,3,0,1:T(8,128)(2,1)} %all-gather.6.cloned.1.call-done) | copy-start | bytes 6291460
  86.8 2.6 %copy-start.3 = (bf16[2,2,512,512]{3,2,0,1:T(8,128)(2,1)S(1)}, bf16[2,2,512,512]{3,2,0,1:T(8,128)(2,1)}, u32[]{:S(2)}) copy-start(bf16[2,2,512,512]{3,2,0,1:T(8,128)(2,1)} %get-tuple-element.9) | copy-start | bytes 6291460
  88.2 2.2 %copy-start.1 = (bf16[2,2,512,512]{2,3,0,1:T(8,128)(2,1)S(1)}, bf16[2,2,512,512]{2,3,0,1:T(8,128)(2,1)}, u32[]{:S(2)}) copy-start(bf16[2,2,512,512]{2,3,0,1:T(8,128)(2,1)} %all-gather.10.cloned.1.call-done) | copy-start | bytes 6291460
  88.2 47.0 %collective-permute-start.2 = (bf16[2,2,512,128]{3,2,0,1:T(8,128)(2,1)}, bf16[2,2,512,128]{3,2,0,1:T(8,128)(2,1)}, u32[]{:S(2)}, u32[]{:S(2)}) collective-permute-start(bf16[2,2,512,128]{3,2,0,1:T(8,128)(2,1)} %pad_maximum_fusion), channel_id=1, source_target_pairs={{0,4},{4,8},{8,12},{12,16},{16,20},{20,24},{24,28},{28,0},{1,5},{5... | collective-permute-start | bytes 1572872 | tf_op jit(solution)/shard_map/ppermute | solution.py:9
  92.5 12.3 %copy-start.8 = (bf16[2,2,512,128]{3,2,1,0:T(8,128)(2,1)S(1)}, bf16[2,2,512,128]{3,2,1,0:T(8,128)(2,1)}, u32[]{:S(2)}) copy-start(bf16[2,2,512,128]{3,2,1,0:T(8,128)(2,1)} %param.4) | copy-start | bytes 1572868
  94.4 40.9 %collective-permute-start.3 = (bf16[2,2,512,128]{3,2,0,1:T(8,128)(2,1)}, bf16[2,2,512,128]{3,2,0,1:T(8,128)(2,1)}, u32[]{:S(2)}, u32[]{:S(2)}) collective-permute-start(bf16[2,2,512,128]{3,2,0,1:T(8,128)(2,1)} %pad_maximum_fusion.1), channel_id=1, source_target_pairs={{0,12},{4,16},{8,20},{12,24},{16,28},{20,0},{24,4},{28,8},{1,13},{... | collective-permute-start | bytes 1572872 | tf_op jit(solution)/shard_map/ppermute | solution.py:9
  104.7 3.6 %copy-start.4 = (bf16[2,2,512,512]{3,2,0,1:T(8,128)(2,1)S(1)}, bf16[2,2,512,512]{3,2,0,1:T(8,128)(2,1)}, u32[]{:S(2)}) copy-start(bf16[2,2,512,512]{3,2,0,1:T(8,128)(2,1)} %get-tuple-element.9) | copy-start | bytes 6291460
  106.5 2.3 %copy-start.12 = (bf16[2,2,512,512]{3,2,0,1:T(8,128)(2,1)S(1)}, bf16[2,2,512,512]{3,2,0,1:T(8,128)(2,1)}, u32[]{:S(2)}) copy-start(bf16[2,2,512,512]{3,2,0,1:T(8,128)(2,1)} %all-gather.12.cloned.1.call-done) | copy-start | bytes 6291460
  129.0 1.8 %copy-start.9 = (bf16[2,2,512,128]{3,2,1,0:T(8,128)(2,1)S(1)}, bf16[2,2,512,128]{3,2,1,0:T(8,128)(2,1)}, u32[]{:S(2)}) copy-start(bf16[2,2,512,128]{3,2,1,0:T(8,128)(2,1)} %param.3) | copy-start | bytes 1572868
  130.8 2.3 %copy-start.13 = (bf16[2,2,512,512]{3,2,0,1:T(8,128)(2,1)S(1)}, bf16[2,2,512,512]{3,2,0,1:T(8,128)(2,1)}, u32[]{:S(2)}) copy-start(bf16[2,2,512,512]{3,2,0,1:T(8,128)(2,1)} %all-gather.8.cloned.1.call-done) | copy-start | bytes 6291460
Sparse Core Ops, SparseCore 0:
  8.9 22.9 all-gather.9
  33.5 22.5 all-gather.5
  57.6 22.8 all-gather.13
  81.9 22.8 all-gather.11
  106.1 22.8 all-gather.7
where the time goes:
time: 147 us; the launch traced here: 144 us
  waiting for transfers between devices  85.7 us (58%)
  matrix products  23.3 us (16%)
  between operations  13.5 us (9%)
  other arithmetic  10.1 us (7%)
  local copies, waits for them, and re-layouts  7.83 us (5%)
  starting transfers between devices  3.82 us (3%)
    ppermute x4, waiting for transfers between devices, from_behind(): lax.ppermute(array, axis, [(i, (i + by) % peers) for i in range(peers)])  38.2 us
    all_gather x1, waiting for transfers between devices, shards(): lax.all_gather(meson, 'col', axis=3, tiled=True)  20.3 us
    all_gather x1, waiting for transfers between devices, shards(): lax.all_gather(shard_ahead_near, 'col', axis=3, tiled=True)  17.9 us
    all_gather x1, waiting for transfers between devices, shards(): lax.all_gather(shard_ahead_far, 'col', axis=3, tiled=True)  9.2 us
    dot_general x8, matrix products, complex_product(): jnp.einsum('tik,tkj->tij', left[:, 0], right[:, 0], preferred_element_typ...  7.86 us
    unnamed x31, local copies, waits for them, and re-layouts  6.8 us
    dot_general x8, matrix products, complex_product(): jnp.einsum('tik,tkj->tij', left[:, 1], right[:, 1], preferred_element_typ...  6.46 us
    dot_general x8, matrix products, complex_product(): jnp.einsum('tik,tkj->tij', left[:, 0], right[:, 1], preferred_element_typ...  5.14 us
  transfers between devices with their start and end apart: 9, of which 5 were waited for; matrix products, arithmetic and copies ran while one was open for 24% of the time, Pallas kernels for 0%

commit v1 on v0

v1 whole, which is shorter than its diff:
```python
import functools

import jax
import jax.numpy as jnp
from jax import lax
from jax.experimental import pallas as pl
from jax.experimental.pallas import tpu as pltpu
from jax.sharding import PartitionSpec as P

MESH = pl.DeviceIdType.MESH
BF16 = jnp.bfloat16
F32 = jnp.float32


def left_form(real, imag):
    top = jnp.concatenate([real, -imag], axis=1)
    low = jnp.concatenate([imag, real], axis=1)
    return jnp.concatenate([top, low], axis=0)


def from_blocks(blocks):
    count = blocks.shape[0]
    real = jnp.concatenate([blocks[j, 0] for j in range(count)], axis=1)
    imag = jnp.concatenate([blocks[j, 1] for j in range(count)], axis=1)
    return left_form(real, imag)


def kernel(
    n_tm, n_col, near, far, meson, out,
    p_in, m_in, a_in, b_out, f_out, b_in, f_in, p_nat, t_nat, i_nat, a_nat,
    p_sem, m_sem, a_sem, b_sem, f_sem, p_send, m_send, b_send, f_send,
):
    order = near.shape[2]
    width = near.shape[3]
    half = order // 2
    tm = lax.axis_index("tm")
    me = lax.axis_index("col")
    y, c = me // 2, me % 2
    step_near, step_far = n_tm // 8, 3 * n_tm // 8
    partner = 2 * y + 1 - c
    across = 2 * (1 - y) + c

    def shifted(by):
        return lax.rem(tm + by + n_tm, n_tm)

    barrier = pltpu.get_barrier_semaphore()
    for d in range(1, n_col):
        pl.semaphore_signal(barrier, inc=1, device_id=(tm, lax.rem(me + d, n_col)), device_id_type=MESH)
    for by in (step_near, -step_near, step_far, -step_far):
        for j in range(n_col):
            pl.semaphore_signal(barrier, inc=1, device_id=(shifted(by), j), device_id_type=MESH)
    pl.semaphore_wait(barrier, n_col - 1 + 4 * n_col)

    def remote(src, dst, send, recv, device):
        return pltpu.make_async_remote_copy(
            src_ref=src, dst_ref=dst, send_sem=send, recv_sem=recv, device_id=device, device_id_type=MESH
        )

    behind_near = (shifted(-step_near), 2 * y)
    behind_far = (shifted(-step_far), 2 * y + 1)

    cross = remote(meson.at[1 - y], m_in.at[me], m_send.at[0], m_sem.at[me], (tm, across))
    cross.start()
    own = [
        remote(meson.at[y], a_in.at[me], m_send.at[1], a_sem.at[me], behind_near),
        remote(meson.at[y], a_in.at[me], m_send.at[2], a_sem.at[me], behind_far),
        remote(meson.at[y], m_in.at[me], m_send.at[3], m_sem.at[me], (tm, partner)),
    ]
    for copy in own:
        copy.start()
    pltpu.make_async_copy(meson.at[y], m_in.at[me], m_sem.at[me]).start()

    def p_copy(target):
        src = (near, far)[target % 2].at[target // 2]
        return remote(src, p_in.at[me], p_send.at[target], p_sem.at[me], (tm, target))

    for target in range(n_col):
        @pl.when(me != target)
        def _():
            p_copy(target).start()

        @pl.when(me == target)
        def _():
            src = (near, far)[target % 2].at[target // 2]
            pltpu.make_async_copy(src, p_in.at[me], p_sem.at[me]).start()

    def arrived(buf, sem, j):
        pltpu.make_async_copy(buf.at[j], buf.at[j], sem.at[j]).wait()

    arrived(m_in, m_sem, across)
    passed = [
        remote(m_in.at[across], m_in.at[across], m_send.at[4], m_sem.at[across], (tm, partner)),
        remote(m_in.at[across], a_in.at[across], m_send.at[5], a_sem.at[across], behind_near),
        remote(m_in.at[across], a_in.at[across], m_send.at[6], a_sem.at[across], behind_far),
    ]
    for copy in passed:
        copy.start()

    for j in range(n_col):
        arrived(p_in, p_sem, j)
    rows = lax.broadcasted_iota(jnp.int32, (order, width), 0)
    for j in range(n_col):
        columns = lax.broadcasted_iota(jnp.int32, (order, width), 1) + j * width
        sign = jnp.where((rows < half) == (columns < half), 1.0, -1.0).astype(F32)
        for part in range(2):
            block = p_in[j, part]
            p_nat[part * order:(part + 1) * order, j * width:(j + 1) * width] = block
            signed = block.astype(F32) * (sign if part == 0 else -sign)
            turned = jnp.transpose(signed).astype(BF16)
            t_nat[part * order + j * width:part * order + (j + 1) * width, :] = turned

    tile = 2 * width

    def product(left, right, store):
        def step(i, carry):
            at = pl.ds(pl.multiple_of(i * tile, tile), tile)
            store(i, at, jnp.dot(left(), right[:, at], preferred_element_type=F32).astype(BF16))
            return carry

        lax.fori_loop(0, order // tile, step, 0)

    def natural(ref):
        def store(i, at, value):
            ref[:, at] = value
        return store

    def blocked(ref):
        def store(i, at, value):
            for k in range(2):
                for part in range(2):
                    ref[2 * i + k, part] = value[part * order:(part + 1) * order, k * width:(k + 1) * width]
        return store

    for d in range(1, n_col):
        arrived(m_in, m_sem, lax.rem(across + d, n_col))

    product(lambda: from_blocks(m_in), t_nat, natural(i_nat))
    product(lambda: from_blocks(p_in), i_nat, blocked(b_out))
    home = jnp.where(c == 0, shifted(step_near), shifted(step_far))
    b_copies = [
        remote(b_out.at[j], b_in.at[c, y], b_send.at[j], b_sem.at[c, y], (home, j)) for j in range(n_col)
    ]
    for copy in b_copies:
        copy.start()

    for j in range(n_col):
        arrived(a_in, a_sem, j)
    product(lambda: from_blocks(a_in), p_nat, natural(a_nat))
    product(lambda: left_form(t_nat[:order, :], t_nat[order:, :]), a_nat, blocked(f_out))

    def f_copy(target):
        return remote(f_out.at[target], f_in.at[c, y], f_send.at[target], f_sem.at[c, y], (tm, target))

    for target in range(n_col):
        @pl.when(me != target)
        def _():
            f_copy(target).start()

        @pl.when(me == target)
        def _():
            pltpu.make_async_copy(f_out.at[target], f_in.at[c, y], f_sem.at[c, y]).start()

    for s in range(2):
        for p in range(2):
            for buf, sem in ((f_in, f_sem), (b_in, b_sem)):
                pltpu.make_async_copy(buf.at[s, p], buf.at[s, p], sem.at[s, p]).wait()
    for p in range(2):
        for part in range(2):
            out[p, part] = (
                f_in[0, p, part].astype(F32) + f_in[1, p, part].astype(F32)
                + b_in[0, p, part].astype(F32) + b_in[1, p, part].astype(F32)
            )

    cross.wait_send()
    for copy in own + passed + b_copies:
        copy.wait_send()
    for target in range(n_col):
        @pl.when(me != target)
        def _():
            p_copy(target).wait_send()
            f_copy(target).wait_send()


def shards(n_tm, n_col, near_prop, far_prop, meson):
    slices, parts, order, width = meson.shape
    blocks = pltpu.VMEM((n_col, parts, order, width), BF16)
    homes = pltpu.VMEM((2, slices, parts, order, width), BF16)
    whole = pltpu.VMEM((parts * order, order), BF16)
    dma = pltpu.SemaphoreType.DMA
    return pl.pallas_call(
        functools.partial(kernel, n_tm, n_col),
        out_shape=jax.ShapeDtypeStruct(meson.shape, F32),
        in_specs=[pl.BlockSpec(memory_space=pl.ANY)] * 3,
        out_specs=pl.BlockSpec(memory_space=pltpu.VMEM),
        scratch_shapes=[
            blocks, blocks, blocks, blocks, blocks, homes, homes, whole, whole, whole, whole,
            dma((n_col,)), dma((n_col,)), dma((n_col,)), dma((2, slices)), dma((2, slices)),
            dma((n_col,)), dma((7,)), dma((n_col,)), dma((n_col,)),
        ],
        compiler_params=pltpu.CompilerParams(
            collective_id=0, has_side_effects=True, vmem_limit_bytes=56 * 1024 * 1024
        ),
    )(near_prop, far_prop, meson)


def solution(mesh):
    spec = P("tm", None, None, "col")
    body = functools.partial(shards, mesh.shape["tm"], mesh.shape["col"])
    return jax.shard_map(body, mesh=mesh, in_specs=(spec, spec, spec), out_specs=spec, check_vma=False)
```

time: 147 us -> 66.3 us (0.45)
  the two profiles are of different devices: /device:TPU:29 before, /device:TPU:15 now
where the time goes in v1:
time: 66.3 us; the launch traced here: 66.1 us
  Pallas kernels  63.9 us (96%)
  local copies, waits for them, and re-layouts  2.26 us (3%)
    pallas_call x1, Pallas kernels, shards(): pl.pallas_call(functools.partial(kernel, n_tm, n_col), out_shape=jax.Shap...  63.9 us
    unnamed x1, local copies, waits for them, and re-layouts  2.26 us

profile of v1, /device:TPU:15, one launch (start us, length us, event | category | flops | bytes accessed | tf_op | source)
XLA Modules:
  0.0 66.1 jit_solution(5970110856560723236)
XLA Ops:
  0.0 63.9 %shard_map.37 = f32[2,2,512,128]{3,2,1,0:T(8,128)} custom-call(bf16[2,2,512,128]{3,2,1,0:T(8,128)(2,1)} %near.1, bf16[2,2,512,128]{3,2,1,0:T(8,128)(2,1)} %far.1, bf16[2,2,512,128]{3,2,1,0:T(8,128)(2,1)} %meson.1), custom_call_target="tpu_custom_call" | custom-call | tf_op jit(solution)/shard_map/pallas_call | solution.py:190
  63.9 2.3 %copy.5 = f32[2,2,512,128]{3,2,1,0:T(8,128)} copy(f32[2,2,512,128]{3,2,1,0:T(8,128)} %shard_map.37) | data formatting | bytes 2097152

commit v2 on v1

v2 whole, which is shorter than its diff:
```python
import functools

import jax
import jax.numpy as jnp
from jax import lax
from jax.experimental import pallas as pl
from jax.experimental.pallas import tpu as pltpu
from jax.sharding import PartitionSpec as P

MESH = pl.DeviceIdType.MESH
BF16 = jnp.bfloat16
F32 = jnp.float32


def left_form(real, imag):
    top = jnp.concatenate([real, -imag], axis=1)
    low = jnp.concatenate([imag, real], axis=1)
    return jnp.concatenate([top, low], axis=0)


def from_blocks(blocks):
    count = blocks.shape[0]
    real = jnp.concatenate([blocks[j, 0] for j in range(count)], axis=1)
    imag = jnp.concatenate([blocks[j, 1] for j in range(count)], axis=1)
    return left_form(real, imag)


def kernel(
    n_tm, n_col, near, far, meson, f_in, b_in,
    p_in, m_in, a_in, b_out, f_out, ra_in, rb_in, p_nat, t_nat,
    p_sem, m_sem, a_sem, b_sem, f_sem, ra_sem, rb_sem, p_send, m_send, b_send, f_send, r_send,
):
    order = near.shape[2]
    width = near.shape[3]
    half = order // 2
    tm = lax.axis_index("tm")
    me = lax.axis_index("col")
    y, c = me // 2, me % 2
    step_near, step_far = n_tm // 8, 3 * n_tm // 8
    partner = 2 * y + 1 - c
    across = 2 * (1 - y) + c
    beyond = 2 * (1 - y) + 1 - c
    relayed = step_near % 2 == 1
    at_x0 = tm % 2 == 0
    tile = 2 * width

    def shifted(by):
        return lax.rem(tm + by + n_tm, n_tm)

    barrier = pltpu.get_barrier_semaphore()
    steps = (step_near, step_far) + ((2 * step_near,) if relayed else ())
    for d in range(1, n_col):
        pl.semaphore_signal(barrier, inc=1, device_id=(tm, lax.rem(me + d, n_col)), device_id_type=MESH)
    for step in steps:
        for by in (step, -step):
            for j in range(n_col):
                pl.semaphore_signal(barrier, inc=1, device_id=(shifted(by), j), device_id_type=MESH)
    pl.semaphore_wait(barrier, n_col - 1 + 2 * len(steps) * n_col)

    def remote(src, dst, send, recv, device):
        return pltpu.make_async_remote_copy(
            src_ref=src, dst_ref=dst, send_sem=send, recv_sem=recv, device_id=device, device_id_type=MESH
        )

    def by_x(at_0, at_1):
        if relayed:
            pl.when(at_x0)(at_0)
            pl.when(jnp.logical_not(at_x0))(at_1)
        else:
            at_1()

    def arrived(buf, sem, j):
        pltpu.make_async_copy(buf.at[j], buf.at[j], sem.at[j]).wait()

    behind_near = (shifted(-step_near), 2 * y)
    behind_far = (shifted(-step_far), 2 * y + 1)

    def ahead_near(src, j, k):
        return remote(src, a_in.at[j], m_send.at[k], a_sem.at[j], behind_near)

    def ahead_near_first(src, k):
        return remote(src, ra_in.at[k], m_send.at[k], ra_sem.at[k], (shifted(-2 * step_near), me))

    def ahead_near_second(k):
        j = (me, across)[k]
        return remote(ra_in.at[k], a_in.at[j], r_send.at[k], a_sem.at[j], behind_mid)

    behind_mid = (shifted(step_near), 2 * y)

    def ahead_far(src, j, k):
        return remote(src, a_in.at[j], m_send.at[2 + k], a_sem.at[j], behind_far)

    def to_partner(src, j, k):
        return remote(src, m_in.at[j], m_send.at[4 + k], m_sem.at[j], (tm, partner))

    def spread(src, j, k):
        by_x(lambda: ahead_near_first(src, k).start(), lambda: ahead_near(src, j, k).start())
        ahead_far(src, j, k).start()
        to_partner(src, j, k).start()

    def p_copy(target):
        src = (near, far)[target % 2].at[target // 2]
        return remote(src, p_in.at[me], p_send.at[target], p_sem.at[me], (tm, target))

    cross = remote(meson.at[1 - y], m_in.at[me], m_send.at[6], m_sem.at[me], (tm, across))
    cross.start()
    spread(meson.at[y], me, 0)
    pltpu.make_async_copy(meson.at[y], m_in.at[me], m_sem.at[me]).start()
    for target in range(n_col):
        @pl.when(me != target)
        def _():
            p_copy(target).start()

        @pl.when(me == target)
        def _():
            src = (near, far)[target % 2].at[target // 2]
            pltpu.make_async_copy(src, p_in.at[me], p_sem.at[me]).start()

    rows = lax.broadcasted_iota(jnp.int32, (order, width), 0)

    def prepare(j):
        arrived(p_in, p_sem, j)
        first = pl.multiple_of(j * width, width)
        columns = lax.broadcasted_iota(jnp.int32, (order, width), 1) + j * width
        sign = jnp.where((rows < half) == (columns < half), 1.0, -1.0).astype(F32)
        for part in range(2):
            block = p_in[j, part]
            p_nat[part * order:(part + 1) * order, pl.ds(first, width)] = block
            signed = block.astype(F32) * (sign if part == 0 else -sign)
            t_nat[pl.ds(part * order + first, width), :] = jnp.transpose(signed).astype(BF16)

    prepare(me)
    prepare(partner)
    arrived(m_in, m_sem, across)
    spread(m_in.at[across], across, 1)
    if relayed:
        @pl.when(at_x0)
        def _():
            for k in range(2):
                arrived(ra_in, ra_sem, k)
                ahead_near_second(k).start()
    prepare(across)
    prepare(beyond)
    for j in (me, partner, beyond):
        arrived(m_in, m_sem, j)

    def product(left, right):
        return jnp.dot(left, right, preferred_element_type=F32).astype(BF16)

    def store(ref, i, value):
        for k in range(2):
            for part in range(2):
                ref[2 * i + k, part] = value[part * order:(part + 1) * order, k * width:(k + 1) * width]

    ahead_by = jnp.where(c == 0, step_near, step_far)
    first_by = jnp.where(c == 0, 2 * step_near, step_far)

    def b_copy(j):
        return remote(b_out.at[j], b_in.at[c, y], b_send.at[j], b_sem.at[c, y], (shifted(ahead_by), j))

    def b_first(j):
        return remote(b_out.at[j], rb_in.at[y], b_send.at[j], rb_sem.at[y], (shifted(2 * step_near), j))

    def b_second(p):
        return remote(rb_in.at[p], b_in.at[0, p], r_send.at[2 + p], b_sem.at[0, p], (shifted(-step_near), me))

    goes_first = jnp.logical_and(c == 0, jnp.logical_not(at_x0))

    def b_send_all(i, act):
        for j in (2 * i, 2 * i + 1):
            if relayed:
                @pl.when(goes_first)
                def _():
                    act(b_first(j))

                @pl.when(jnp.logical_not(goes_first))
                def _():
                    act(b_copy(j))
            else:
                act(b_copy(j))

    for i in range(order // tile):
        at = pl.ds(i * tile, tile)
        inner = product(from_blocks(m_in), t_nat[:, at])
        store(b_out, i, product(from_blocks(p_in), inner))
        b_send_all(i, lambda copy: copy.start())

    for j in range(n_col):
        arrived(a_in, a_sem, j)

    def f_copy(target):
        return remote(f_out.at[target], f_in.at[c, y], f_send.at[target], f_sem.at[c, y], (tm, target))

    for i in range(order // tile):
        at = pl.ds(i * tile, tile)
        ahead = product(from_blocks(a_in), p_nat[:, at])
        store(f_out, i, product(left_form(t_nat[:order, :], t_nat[order:, :]), ahead))
        for target in (2 * i, 2 * i + 1):
            @pl.when(me != target)
            def _():
                f_copy(target).start()

            @pl.when(me == target)
            def _():
                pltpu.make_async_copy(f_out.at[target], f_in.at[c, y], f_sem.at[c, y]).start()

    if relayed:
        @pl.when(jnp.logical_not(at_x0))
        def _():
            for p in (y, 1 - y):
                arrived(rb_in, rb_sem, p)
                b_second(p).start()

    for s in range(2):
        for p in range(2):
            for buf, sem in ((f_in, f_sem), (b_in, b_sem)):
                pltpu.make_async_copy(buf.at[s, p], buf.at[s, p], sem.at[s, p]).wait()

    cross.wait_send()
    for k in range(2):
        src, j = ((meson.at[y], me), (m_in.at[across], across))[k]
        by_x(lambda: ahead_near_first(src, k).wait_send(), lambda: ahead_near(src, j, k).wait_send())
        ahead_far(src, j, k).wait_send()
        to_partner(src, j, k).wait_send()
    if relayed:
        @pl.when(at_x0)
        def _():
            for k in range(2):
                ahead_near_second(k).wait_send()

        @pl.when(jnp.logical_not(at_x0))
        def _():
            for p in (y, 1 - y):
                b_second(p).wait_send()
    for i in range(order // tile):
        b_send_all(i, lambda copy: copy.wait_send())
    for target in range(n_col):
        @pl.when(me != target)
        def _():
            p_copy(target).wait_send()
            f_copy(target).wait_send()


def shards(n_tm, n_col, near_prop, far_prop, meson):
    slices, parts, order, width = meson.shape
    blocks = pltpu.VMEM((n_col, parts, order, width), BF16)
    pair = pltpu.VMEM((2, parts, order, width), BF16)
    whole = pltpu.VMEM((parts * order, order), BF16)
    home = jax.ShapeDtypeStruct((2, slices, parts, order, width), BF16)
    dma = pltpu.SemaphoreType.DMA
    forward, backward = pl.pallas_call(
        functools.partial(kernel, n_tm, n_col),
        out_shape=(home, home),
        in_specs=[pl.BlockSpec(memory_space=pl.ANY)] * 3,
        out_specs=[pl.BlockSpec(memory_space=pl.ANY)] * 2,
        scratch_shapes=[
            blocks, blocks, blocks, blocks, blocks, pair, pair, whole, whole,
            dma((n_col,)), dma((n_col,)), dma((n_col,)), dma((2, slices)), dma((2, slices)), dma((2,)), dma((2,)),
            dma((n_col,)), dma((7,)), dma((n_col,)), dma((n_col,)), dma((4,)),
        ],
        compiler_params=pltpu.CompilerParams(
            collective_id=0, has_side_effects=True, vmem_limit_bytes=56 * 1024 * 1024
        ),
    )(near_prop, far_prop, meson)
    forward, backward = forward.astype(F32), backward.astype(F32)
    return forward[0] + forward[1] + backward[0] + backward[1]


def solution(mesh):
    spec = P("tm", None, None, "col")
    body = functools.partial(shards, mesh.shape["tm"], mesh.shape["col"])
    return jax.shard_map(body, mesh=mesh, in_specs=(spec, spec, spec), out_specs=spec, check_vma=False)
```

time: 66.3 us -> 72.5 us (1.094)
  Pallas kernels: 63.9 us -> 69.5 us
  other arithmetic: 0 us -> 2.74 us
  local copies, waits for them, and re-layouts: 2.26 us -> 0.08 us
    pallas_call x1, Pallas kernels: 63.9 us -> 69.5 us  [shards(): pl.pallas_call(functools.partial(kernel, n_tm, n_col), out_shape=(home, h...]
    unnamed x1 -> x2, local copies, waits for them, and re-layouts: 2.26 us -> 0.08 us
    convert_element_type x0 -> x2, other arithmetic: none -> 1.59 us  [shards(): forward, backward = (forward.astype(F32), backward.astype(F32))]
    add x0 -> x1, other arithmetic: none -> 1.16 us  [shards(): return forward[0] + forward[1] + backward[0] + backward[1]]
where the time goes in v2:
time: 72.5 us; the launch traced here: 72.4 us
  Pallas kernels  69.5 us (96%)
  other arithmetic  2.74 us (4%)
    pallas_call x1, Pallas kernels, shards(): pl.pallas_call(functools.partial(kernel, n_tm, n_col), out_shape=(home, h...  69.5 us
    convert_element_type x2, other arithmetic, shards(): forward, backward = (forward.astype(F32), backward.astype(F32))  1.59 us

profile of v2, /device:TPU:15, one launch (start us, length us, event | category | flops | bytes accessed | tf_op | source)
XLA Modules:
  0.0 72.4 jit_solution(5774272451281428210)
XLA Ops:
  0.0 69.5 %shard_map.37 = (bf16[2,2,2,512,128]{4,3,2,1,0:T(8,128)(2,1)}, bf16[2,2,2,512,128]{4,3,2,1,0:T(8,128)(2,1)}) custom-call(bf16[2,2,512,128]{3,2,1,0:T(8,128)(2,1)} %near.1, bf16[2,2,512,128]{3,2,1,0:T(8,128)(2,1)} %far.1, bf16[2,2,512,128]{3,2,1,0:T(8,128)(2,1)} %meson.1), custom_call_target="tpu_custom_call" | custom-call | tf_op jit(solution)/shard_map/pallas_call | solution.py:251
  69.5 0.0 copy-start
  69.5 1.4 %convert_element_type.6 = f32[2,2,2,512,128]{4,3,2,1,0:T(8,128)S(1)} convert(bf16[2,2,2,512,128]{4,3,2,1,0:T(8,128)(2,1)} %get-tuple-element.7) | non-fusion elementwise | flops 524288 | bytes 3145728 | tf_op jit(solution)/shard_map/convert_element_type | solution.py:265
  71.0 0.1 copy-done
  71.1 0.1 convert_element_type.7
  71.2 1.2 %fusion = f32[2,2,512,128]{3,2,1,0:T(8,128)} fusion(f32[2,2,2,512,128]{4,3,2,1,0:T(8,128)S(1)} %convert_element_type.7, f32[2,2,2,512,128]{4,3,2,1,0:T(8,128)S(1)} %convert_element_type.6), kind=kLoop, calls=%fused_computation.1 | loop fusion | flops 786432 | bytes 5242880 | tf_op jit(solution)/shard_map/add | solution.py:266
Async XLA Ops:
  69.5 1.5 %copy-start = (bf16[2,2,2,512,128]{4,3,2,1,0:T(8,128)(2,1)S(1)}, bf16[2,2,2,512,128]{4,3,2,1,0:T(8,128)(2,1)}, u32[]{:S(2)}) copy-start(bf16[2,2,2,512,128]{4,3,2,1,0:T(8,128)(2,1)} %get-tuple-element.8) | copy-start | bytes 3145732

commit v3 on v2

--- a/solution.py
+++ b/solution.py
@@ -41,7 +41,7 @@
     across = 2 * (1 - y) + c
     beyond = 2 * (1 - y) + 1 - c
     relayed = step_near % 2 == 1
-    at_x0 = tm % 2 == 0
+    at_x0, at_x1 = tm % 2 == 0, tm % 2 == 1
     tile = 2 * width
 
     def shifted(by):
@@ -65,7 +65,7 @@
     def by_x(at_0, at_1):
         if relayed:
             pl.when(at_x0)(at_0)
-            pl.when(jnp.logical_not(at_x0))(at_1)
+            pl.when(at_x1)(at_1)
         else:
             at_1()
 
@@ -79,13 +79,13 @@
         return remote(src, a_in.at[j], m_send.at[k], a_sem.at[j], behind_near)
 
     def ahead_near_first(src, k):
-        return remote(src, ra_in.at[k], m_send.at[k], ra_sem.at[k], (shifted(-2 * step_near), me))
+        return remote(src, ra_in.at[k], m_send.at[k], ra_sem.at[k], (shifted(step_near), me))
 
     def ahead_near_second(k):
         j = (me, across)[k]
         return remote(ra_in.at[k], a_in.at[j], r_send.at[k], a_sem.at[j], behind_mid)
 
-    behind_mid = (shifted(step_near), 2 * y)
+    behind_mid = (shifted(-2 * step_near), 2 * y)
 
     def ahead_far(src, j, k):
         return remote(src, a_in.at[j], m_send.at[2 + k], a_sem.at[j], behind_far)
@@ -134,7 +134,7 @@
     arrived(m_in, m_sem, across)
     spread(m_in.at[across], across, 1)
     if relayed:
-        @pl.when(at_x0)
+        @pl.when(at_x1)
         def _():
             for k in range(2):
                 arrived(ra_in, ra_sem, k)
@@ -153,18 +153,17 @@
                 ref[2 * i + k, part] = value[part * order:(part + 1) * order, k * width:(k + 1) * width]
 
     ahead_by = jnp.where(c == 0, step_near, step_far)
-    first_by = jnp.where(c == 0, 2 * step_near, step_far)
 
     def b_copy(j):
         return remote(b_out.at[j], b_in.at[c, y], b_send.at[j], b_sem.at[c, y], (shifted(ahead_by), j))
 
     def b_first(j):
-        return remote(b_out.at[j], rb_in.at[y], b_send.at[j], rb_sem.at[y], (shifted(2 * step_near), j))
+        return remote(b_out.at[j], rb_in.at[y], b_send.at[j], rb_sem.at[y], (shifted(-step_near), j))
 
     def b_second(p):
-        return remote(rb_in.at[p], b_in.at[0, p], r_send.at[2 + p], b_sem.at[0, p], (shifted(-step_near), me))
-
-    goes_first = jnp.logical_and(c == 0, jnp.logical_not(at_x0))
+        return remote(rb_in.at[p], b_in.at[0, p], r_send.at[2 + p], b_sem.at[0, p], (shifted(2 * step_near), me))
+
+    goes_first = jnp.logical_and(c == 0, at_x1)
 
     def b_send_all(i, act):
         for j in (2 * i, 2 * i + 1):
@@ -205,7 +204,7 @@
                 pltpu.make_async_copy(f_out.at[target], f_in.at[c, y], f_sem.at[c, y]).start()
 
     if relayed:
-        @pl.when(jnp.logical_not(at_x0))
+        @pl.when(at_x0)
         def _():
             for p in (y, 1 - y):
                 arrived(rb_in, rb_sem, p)
@@ -223,12 +222,12 @@
         ahead_far(src, j, k).wait_send()
         to_partner(src, j, k).wait_send()
     if relayed:
-        @pl.when(at_x0)
+        @pl.when(at_x1)
         def _():
             for k in range(2):
                 ahead_near_second(k).wait_send()
 
-        @pl.when(jnp.logical_not(at_x0))
+        @pl.when(at_x0)
         def _():
             for p in (y, 1 - y):
                 b_second(p).wait_send()
@@ -262,8 +261,8 @@
             collective_id=0, has_side_effects=True, vmem_limit_bytes=56 * 1024 * 1024
         ),
     )(near_prop, far_prop, meson)
-    forward, backward = forward.astype(F32), backward.astype(F32)
-    return forward[0] + forward[1] + backward[0] + backward[1]
+    terms = [array[s].astype(F32) for array in (forward, backward) for s in range(2)]
+    return terms[0] + terms[1] + terms[2] + terms[3]
 
 
 def solution(mesh):

time: 72.5 us -> 66.9 us (0.923)
  the two profiles are of different devices: /device:TPU:15 before, /device:TPU:29 now
where the time goes in v3:
time: 66.9 us; the launch traced here: 66.7 us
  Pallas kernels  64 us (96%)
  other arithmetic  2.73 us (4%)
    pallas_call x1, Pallas kernels, shards(): pl.pallas_call(functools.partial(kernel, n_tm, n_col), out_shape=(home, h...  64 us
    add x1, other arithmetic, shards(): return terms[0] + terms[1] + terms[2] + terms[3]  2.73 us

profile of v3, /device:TPU:29, one launch (start us, length us, event | category | flops | bytes accessed | tf_op | source)
XLA Modules:
  0.0 66.7 jit_solution(7145647954184842557)
XLA Ops:
  0.0 64.0 %shard_map.37 = (bf16[2,2,2,512,128]{4,3,2,1,0:T(8,128)(2,1)}, bf16[2,2,2,512,128]{4,3,2,1,0:T(8,128)(2,1)}) custom-call(bf16[2,2,512,128]{3,2,1,0:T(8,128)(2,1)} %near.1, bf16[2,2,512,128]{3,2,1,0:T(8,128)(2,1)} %far.1, bf16[2,2,512,128]{3,2,1,0:T(8,128)(2,1)} %meson.1), custom_call_target="tpu_custom_call" | custom-call | tf_op jit(solution)/shard_map/pallas_call | solution.py:250
  64.0 2.7 %add_bitcast_fusion = f32[2,2,512,128]{3,2,1,0:T(8,128)} fusion(bf16[2,2,2,512,128]{4,3,2,1,0:T(8,128)(2,1)} %get-tuple-element.8, bf16[2,2,2,512,128]{4,3,2,1,0:T(8,128)(2,1)} %get-tuple-element.7), kind=kLoop, calls=%fused_computation | loop fusion | flops 1835008 | bytes 3145728 | tf_op jit(solution)/shard_map/add | solution.py:265

commit v4 on v3

v4 whole, which is shorter than its diff:
```python
import functools

import jax
import jax.numpy as jnp
from jax import lax
from jax.experimental import pallas as pl
from jax.experimental.pallas import tpu as pltpu
from jax.sharding import PartitionSpec as P

MESH = pl.DeviceIdType.MESH
BF16 = jnp.bfloat16
F32 = jnp.float32


def left_form(real, imag):
    top = jnp.concatenate([real, -imag], axis=1)
    low = jnp.concatenate([imag, real], axis=1)
    return jnp.concatenate([top, low], axis=0)


def from_blocks(blocks):
    count = blocks.shape[0]
    real = jnp.concatenate([blocks[j, 0] for j in range(count)], axis=1)
    imag = jnp.concatenate([blocks[j, 1] for j in range(count)], axis=1)
    return left_form(real, imag)


def kernel(
    n_tm, n_col, near, far, meson, f_in, b_in,
    p_in, m_in, a_in, b_out, f_out, bf_in, p_nat, t_nat,
    p_sem, m_sem, a_sem, b_sem, f_sem, bf_sem, p_send, m_send, a_send, b_send, f_send,
):
    order = near.shape[2]
    width = near.shape[3]
    half = order // 2
    tm = lax.axis_index("tm")
    me = lax.axis_index("col")
    y, c = me // 2, me % 2
    step_near, step_far = n_tm // 8, 3 * n_tm // 8
    partner = 2 * y + 1 - c
    across = 2 * (1 - y) + c
    beyond = 2 * (1 - y) + 1 - c
    between = step_far - step_near
    tile = 2 * width

    def shifted(by):
        return lax.rem(tm + by + n_tm, n_tm)

    barrier = pltpu.get_barrier_semaphore()
    steps = (step_near, between)
    for d in range(1, n_col):
        pl.semaphore_signal(barrier, inc=1, device_id=(tm, lax.rem(me + d, n_col)), device_id_type=MESH)
    for step in steps:
        for by in (step, -step):
            for j in range(n_col):
                pl.semaphore_signal(barrier, inc=1, device_id=(shifted(by), j), device_id_type=MESH)
    pl.semaphore_wait(barrier, n_col - 1 + 2 * len(steps) * n_col)

    def remote(src, dst, send, recv, device):
        return pltpu.make_async_remote_copy(
            src_ref=src, dst_ref=dst, send_sem=send, recv_sem=recv, device_id=device, device_id_type=MESH
        )

    def arrived(buf, sem, j):
        pltpu.make_async_copy(buf.at[j], buf.at[j], sem.at[j]).wait()

    def ahead_near(src, j, k):
        device = (shifted(-step_near), 2 * y)
        return remote(src, a_in.at[j], m_send.at[k], a_sem.at[j], device)

    def ahead_far(j):
        device = (shifted(-between), 2 * y + 1)
        return remote(a_in.at[j], a_in.at[j], a_send.at[j], a_sem.at[j], device)

    def to_partner(src, j, k):
        return remote(src, m_in.at[j], m_send.at[2 + k], m_sem.at[j], (tm, partner))

    def spread(src, j, k):
        ahead_near(src, j, k).start()
        to_partner(src, j, k).start()

    def p_copy(target):
        src = (near, far)[target % 2].at[target // 2]
        return remote(src, p_in.at[me], p_send.at[target], p_sem.at[me], (tm, target))

    cross = remote(meson.at[1 - y], m_in.at[me], m_send.at[4], m_sem.at[me], (tm, across))
    cross.start()
    spread(meson.at[y], me, 0)
    pltpu.make_async_copy(meson.at[y], m_in.at[me], m_sem.at[me]).start()
    for target in range(n_col):
        @pl.when(me != target)
        def _():
            p_copy(target).start()

        @pl.when(me == target)
        def _():
            src = (near, far)[target % 2].at[target // 2]
            pltpu.make_async_copy(src, p_in.at[me], p_sem.at[me]).start()

    rows = lax.broadcasted_iota(jnp.int32, (order, width), 0)

    def prepare(j):
        arrived(p_in, p_sem, j)
        first = pl.multiple_of(j * width, width)
        columns = lax.broadcasted_iota(jnp.int32, (order, width), 1) + j * width
        sign = jnp.where((rows < half) == (columns < half), 1.0, -1.0).astype(F32)
        for part in range(2):
            block = p_in[j, part]
            p_nat[part * order:(part + 1) * order, pl.ds(first, width)] = block
            signed = block.astype(F32) * (sign if part == 0 else -sign)
            t_nat[pl.ds(part * order + first, width), :] = jnp.transpose(signed).astype(BF16)

    prepare(me)
    prepare(partner)
    arrived(m_in, m_sem, across)
    spread(m_in.at[across], across, 1)

    @pl.when(c == 0)
    def _():
        for j in (me, partner, across, beyond):
            arrived(a_in, a_sem, j)
            ahead_far(j).start()

    prepare(across)
    prepare(beyond)
    for j in (me, partner, beyond):
        arrived(m_in, m_sem, j)

    def product(left, right):
        return jnp.dot(left, right, preferred_element_type=F32).astype(BF16)

    def store(ref, i, value):
        for k in range(2):
            for part in range(2):
                ref[2 * i + k, part] = value[part * order:(part + 1) * order, k * width:(k + 1) * width]

    def b_far(j):
        return remote(b_out.at[j], bf_in.at[j], b_send.at[j], bf_sem.at[j], (shifted(between), 2 * y))

    def b_home(j):
        return remote(b_out.at[j], b_in.at[y], b_send.at[j], b_sem.at[y], (shifted(step_near), j))

    for i in range(order // tile):
        at = pl.ds(i * tile, tile)
        inner = product(from_blocks(m_in), t_nat[:, at])
        store(b_out, i, product(from_blocks(p_in), inner))

        @pl.when(c == 1)
        def _():
            for j in (2 * i, 2 * i + 1):
                b_far(j).start()

    @pl.when(c == 1)
    def _():
        for j in range(n_col):
            arrived(a_in, a_sem, j)

    def f_copy(target):
        return remote(f_out.at[target], f_in.at[c, y], f_send.at[target], f_sem.at[c, y], (tm, target))

    for i in range(order // tile):
        at = pl.ds(i * tile, tile)
        ahead = product(from_blocks(a_in), p_nat[:, at])
        store(f_out, i, product(left_form(t_nat[:order, :], t_nat[order:, :]), ahead))
        for target in (2 * i, 2 * i + 1):
            @pl.when(me != target)
            def _():
                f_copy(target).start()

            @pl.when(me == target)
            def _():
                pltpu.make_async_copy(f_out.at[target], f_in.at[c, y], f_sem.at[c, y]).start()

    @pl.when(c == 0)
    def _():
        for j in range(n_col):
            arrived(bf_in, bf_sem, j)
            b_out[j] = (b_out[j].astype(F32) + bf_in[j].astype(F32)).astype(BF16)
            b_home(j).start()

    for p in range(2):
        for s in range(2):
            pltpu.make_async_copy(f_in.at[s, p], f_in.at[s, p], f_sem.at[s, p]).wait()
        arrived(b_in, b_sem, p)

    cross.wait_send()
    for k in range(2):
        src, j = ((meson.at[y], me), (m_in.at[across], across))[k]
        ahead_near(src, j, k).wait_send()
        to_partner(src, j, k).wait_send()

    @pl.when(c == 0)
    def _():
        for j in range(n_col):
            ahead_far(j).wait_send()
            b_home(j).wait_send()

    @pl.when(c == 1)
    def _():
        for j in range(n_col):
            b_far(j).wait_send()

    for target in range(n_col):
        @pl.when(me != target)
        def _():
            p_copy(target).wait_send()
            f_copy(target).wait_send()


def shards(n_tm, n_col, near_prop, far_prop, meson):
    slices, parts, order, width = meson.shape
    blocks = pltpu.VMEM((n_col, parts, order, width), BF16)
    whole = pltpu.VMEM((parts * order, order), BF16)
    home = jax.ShapeDtypeStruct((slices, parts, order, width), BF16)
    homes = jax.ShapeDtypeStruct((2, slices, parts, order, width), BF16)
    dma = pltpu.SemaphoreType.DMA
    forward, backward = pl.pallas_call(
        functools.partial(kernel, n_tm, n_col),
        out_shape=(homes, home),
        in_specs=[pl.BlockSpec(memory_space=pl.ANY)] * 3,
        out_specs=[pl.BlockSpec(memory_space=pl.ANY)] * 2,
        scratch_shapes=[
            blocks, blocks, blocks, blocks, blocks, blocks, whole, whole,
            dma((n_col,)), dma((n_col,)), dma((n_col,)), dma((slices,)), dma((2, slices)), dma((n_col,)),
            dma((n_col,)), dma((5,)), dma((n_col,)), dma((n_col,)), dma((n_col,)),
        ],
        compiler_params=pltpu.CompilerParams(
            collective_id=0, has_side_effects=True, vmem_limit_bytes=56 * 1024 * 1024
        ),
    )(near_prop, far_prop, meson)
    return forward[0].astype(F32) + forward[1].astype(F32) + backward.astype(F32)


def solution(mesh):
    spec = P("tm", None, None, "col")
    body = functools.partial(shards, mesh.shape["tm"], mesh.shape["col"])
    return jax.shard_map(body, mesh=mesh, in_specs=(spec, spec, spec), out_specs=spec, check_vma=False)
```

time: 66.9 us -> 57.4 us (0.86)
  the two profiles are of different devices: /device:TPU:29 before, /device:TPU:13 now
where the time goes in v4:
time: 57.4 us; the launch traced here: 57.3 us
  Pallas kernels  54.8 us (95%)
  other arithmetic  2.5 us (4%)
    pallas_call x1, Pallas kernels, shards(): pl.pallas_call(functools.partial(kernel, n_tm, n_col), out_shape=(homes,...  54.8 us
    add x1, other arithmetic, shards(): forward[0].astype(F32) + forward[1].astype(F32) + backward.astype(F32)  2.5 us

profile of v4, /device:TPU:13, one launch (start us, length us, event | category | flops | bytes accessed | tf_op | source)
XLA Modules:
  0.0 57.3 jit_solution(16133605227700021501)
XLA Ops:
  0.0 54.8 %shard_map.37 = (bf16[2,2,2,512,128]{4,3,2,1,0:T(8,128)(2,1)}, bf16[2,2,512,128]{3,2,1,0:T(8,128)(2,1)}) custom-call(bf16[2,2,512,128]{3,2,1,0:T(8,128)(2,1)} %near.1, bf16[2,2,512,128]{3,2,1,0:T(8,128)(2,1)} %far.1, bf16[2,2,512,128]{3,2,1,0:T(8,128)(2,1)} %meson.1), custom_call_target="tpu_custom_call" | custom-call | tf_op jit(solution)/shard_map/pallas_call | solution.py:217
  54.8 2.5 %bitcast_add_fusion = f32[2,2,512,128]{3,2,1,0:T(8,128)} fusion(bf16[2,2,512,128]{3,2,1,0:T(8,128)(2,1)} %get-tuple-element.8, bf16[2,2,2,512,128]{4,3,2,1,0:T(8,128)(2,1)} %get-tuple-element.7), kind=kLoop, calls=%fused_computation | loop fusion | flops 1310720 | bytes 2621440 | tf_op jit(solution)/shard_map/add | solution.py:231

commit v5 on v4

--- a/solution.py
+++ b/solution.py
@@ -87,7 +87,7 @@
     cross.start()
     spread(meson.at[y], me, 0)
     pltpu.make_async_copy(meson.at[y], m_in.at[me], m_sem.at[me]).start()
-    for target in range(n_col):
+    for target in tuple(range(1, n_col, 2)) + tuple(range(0, n_col, 2)):
         @pl.when(me != target)
         def _():
             p_copy(target).start()
@@ -150,6 +150,16 @@
             for j in (2 * i, 2 * i + 1):
                 b_far(j).start()
 
+    def join(blocks):
+        @pl.when(c == 0)
+        def _():
+            for j in blocks:
+                arrived(bf_in, bf_sem, j)
+                b_out[j] = (b_out[j].astype(F32) + bf_in[j].astype(F32)).astype(BF16)
+                b_home(j).start()
+
+    join((0, 1))
+
     @pl.when(c == 1)
     def _():
         for j in range(n_col):
@@ -171,12 +181,7 @@
             def _():
                 pltpu.make_async_copy(f_out.at[target], f_in.at[c, y], f_sem.at[c, y]).start()
 
-    @pl.when(c == 0)
-    def _():
-        for j in range(n_col):
-            arrived(bf_in, bf_sem, j)
-            b_out[j] = (b_out[j].astype(F32) + bf_in[j].astype(F32)).astype(BF16)
-            b_home(j).start()
+        join((2 + i,))
 
     for p in range(2):
         for s in range(2):

time: 57.4 us -> 62.3 us (1.085)
  the two profiles are of different devices: /device:TPU:13 before, /device:TPU:29 now
where the time goes in v5:
time: 62.3 us; the launch traced here: 62.2 us
  Pallas kernels  59.6 us (96%)
  other arithmetic  2.5 us (4%)
    pallas_call x1, Pallas kernels, shards(): pl.pallas_call(functools.partial(kernel, n_tm, n_col), out_shape=(homes,...  59.6 us
    add x1, other arithmetic, shards(): forward[0].astype(F32) + forward[1].astype(F32) + backward.astype(F32)  2.5 us

profile of v5, /device:TPU:29, one launch (start us, length us, event | category | flops | bytes accessed | tf_op | source)
XLA Modules:
  0.0 62.2 jit_solution(15067472057501000462)
XLA Ops:
  0.0 59.6 %shard_map.37 = (bf16[2,2,2,512,128]{4,3,2,1,0:T(8,128)(2,1)}, bf16[2,2,512,128]{3,2,1,0:T(8,128)(2,1)}) custom-call(bf16[2,2,512,128]{3,2,1,0:T(8,128)(2,1)} %near.1, bf16[2,2,512,128]{3,2,1,0:T(8,128)(2,1)} %far.1, bf16[2,2,512,128]{3,2,1,0:T(8,128)(2,1)} %meson.1), custom_call_target="tpu_custom_call" | custom-call | tf_op jit(solution)/shard_map/pallas_call | solution.py:222
  59.7 2.5 %bitcast_add_fusion = f32[2,2,512,128]{3,2,1,0:T(8,128)} fusion(bf16[2,2,512,128]{3,2,1,0:T(8,128)(2,1)} %get-tuple-element.8, bf16[2,2,2,512,128]{4,3,2,1,0:T(8,128)(2,1)} %get-tuple-element.7), kind=kLoop, calls=%fused_computation | loop fusion | flops 1310720 | bytes 2621440 | tf_op jit(solution)/shard_map/add | solution.py:236

commit v6 on v5

--- a/solution.py
+++ b/solution.py
@@ -41,13 +41,15 @@
     across = 2 * (1 - y) + c
     beyond = 2 * (1 - y) + 1 - c
     between = step_far - step_near
+    odd = step_near % 2 == 1
+    at_x0, at_x1 = tm % 2 == 0, tm % 2 == 1
     tile = 2 * width
 
     def shifted(by):
         return lax.rem(tm + by + n_tm, n_tm)
 
     barrier = pltpu.get_barrier_semaphore()
-    steps = (step_near, between)
+    steps = (step_near, between) + ((step_far,) if odd else ())
     for d in range(1, n_col):
         pl.semaphore_signal(barrier, inc=1, device_id=(tm, lax.rem(me + d, n_col)), device_id_type=MESH)
     for step in steps:
@@ -72,6 +74,10 @@
         device = (shifted(-between), 2 * y + 1)
         return remote(a_in.at[j], a_in.at[j], a_send.at[j], a_sem.at[j], device)
 
+    def ahead_direct():
+        device = (shifted(-step_far), 2 * y + 1)
+        return remote(meson.at[y], a_in.at[me], m_send.at[5], a_sem.at[me], device)
+
     def to_partner(src, j, k):
         return remote(src, m_in.at[j], m_send.at[2 + k], m_sem.at[j], (tm, partner))
 
@@ -86,6 +92,11 @@
     cross = remote(meson.at[1 - y], m_in.at[me], m_send.at[4], m_sem.at[me], (tm, across))
     cross.start()
     spread(meson.at[y], me, 0)
+    if odd:
+        @pl.when(at_x1)
+        def _():
+            ahead_direct().start()
+
     pltpu.make_async_copy(meson.at[y], m_in.at[me], m_sem.at[me]).start()
     for target in tuple(range(1, n_col, 2)) + tuple(range(0, n_col, 2)):
         @pl.when(me != target)
@@ -117,7 +128,15 @@
 
     @pl.when(c == 0)
     def _():
-        for j in (me, partner, across, beyond):
+        for j in (me, partner):
+            arrived(a_in, a_sem, j)
+            if odd:
+                @pl.when(at_x1)
+                def _():
+                    ahead_far(j).start()
+            else:
+                ahead_far(j).start()
+        for j in (across, beyond):
             arrived(a_in, a_sem, j)
             ahead_far(j).start()
 
@@ -158,7 +177,6 @@
                 b_out[j] = (b_out[j].astype(F32) + bf_in[j].astype(F32)).astype(BF16)
                 b_home(j).start()
 
-    join((0, 1))
 
     @pl.when(c == 1)
     def _():
@@ -181,7 +199,7 @@
             def _():
                 pltpu.make_async_copy(f_out.at[target], f_in.at[c, y], f_sem.at[c, y]).start()
 
-        join((2 + i,))
+        join((0,) if i == 0 else (1, 2, 3))
 
     for p in range(2):
         for s in range(2):
@@ -189,6 +207,11 @@
         arrived(b_in, b_sem, p)
 
     cross.wait_send()
+    if odd:
+        @pl.when(at_x1)
+        def _():
+            ahead_direct().wait_send()
+
     for k in range(2):
         src, j = ((meson.at[y], me), (m_in.at[across], across))[k]
         ahead_near(src, j, k).wait_send()
@@ -196,8 +219,16 @@
 
     @pl.when(c == 0)
     def _():
+        for j in (me, partner):
+            if odd:
+                @pl.when(at_x1)
+                def _():
+                    ahead_far(j).wait_send()
+            else:
+                ahead_far(j).wait_send()
+        for j in (across, beyond):
+            ahead_far(j).wait_send()
         for j in range(n_col):
-            ahead_far(j).wait_send()
             b_home(j).wait_send()
 
     @pl.when(c == 1)
@@ -227,7 +258,7 @@
         scratch_shapes=[
             blocks, blocks, blocks, blocks, blocks, blocks, whole, whole,
             dma((n_col,)), dma((n_col,)), dma((n_col,)), dma((slices,)), dma((2, slices)), dma((n_col,)),
-            dma((n_col,)), dma((5,)), dma((n_col,)), dma((n_col,)), dma((n_col,)),
+            dma((n_col,)), dma((6,)), dma((n_col,)), dma((n_col,)), dma((n_col,)),
         ],
         compiler_params=pltpu.CompilerParams(
             collective_id=0, has_side_effects=True, vmem_limit_bytes=56 * 1024 * 1024

time: 62.3 us -> 57.9 us (0.929)
  Pallas kernels: 59.6 us -> 54.9 us
    pallas_call x1, Pallas kernels: 59.6 us -> 54.9 us  [shards(): pl.pallas_call(functools.partial(kernel, n_tm, n_col), out_shape=(homes,...]
where the time goes in v6:
time: 57.9 us; the launch traced here: 57.4 us
  Pallas kernels  54.9 us (95%)
  other arithmetic  2.5 us (4%)
    pallas_call x1, Pallas kernels, shards(): pl.pallas_call(functools.partial(kernel, n_tm, n_col), out_shape=(homes,...  54.9 us
    add x1, other arithmetic, shards(): forward[0].astype(F32) + forward[1].astype(F32) + backward.astype(F32)  2.5 us

profile of v6, /device:TPU:29, one launch (start us, length us, event | category | flops | bytes accessed | tf_op | source)
XLA Modules:
  0.0 57.4 jit_solution(1544190986457604684)
XLA Ops:
  0.0 54.9 %shard_map.37 = (bf16[2,2,2,512,128]{4,3,2,1,0:T(8,128)(2,1)}, bf16[2,2,512,128]{3,2,1,0:T(8,128)(2,1)}) custom-call(bf16[2,2,512,128]{3,2,1,0:T(8,128)(2,1)} %near.1, bf16[2,2,512,128]{3,2,1,0:T(8,128)(2,1)} %far.1, bf16[2,2,512,128]{3,2,1,0:T(8,128)(2,1)} %meson.1), custom_call_target="tpu_custom_call" | custom-call | tf_op jit(solution)/shard_map/pallas_call | solution.py:253
  54.9 2.5 %bitcast_add_fusion = f32[2,2,512,128]{3,2,1,0:T(8,128)} fusion(bf16[2,2,512,128]{3,2,1,0:T(8,128)(2,1)} %get-tuple-element.8, bf16[2,2,2,512,128]{4,3,2,1,0:T(8,128)(2,1)} %get-tuple-element.7), kind=kLoop, calls=%fused_computation | loop fusion | flops 1310720 | bytes 2621440 | tf_op jit(solution)/shard_map/add | solution.py:267

commit v7 on v5

--- a/solution.py
+++ b/solution.py
@@ -158,7 +158,6 @@
                 b_out[j] = (b_out[j].astype(F32) + bf_in[j].astype(F32)).astype(BF16)
                 b_home(j).start()
 
-    join((0, 1))
 
     @pl.when(c == 1)
     def _():
@@ -181,7 +180,7 @@
             def _():
                 pltpu.make_async_copy(f_out.at[target], f_in.at[c, y], f_sem.at[c, y]).start()
 
-        join((2 + i,))
+        join((0,) if i == 0 else (1, 2, 3))
 
     for p in range(2):
         for s in range(2):

time: 62.3 us -> 57.4 us (0.921)
  Pallas kernels: 59.6 us -> 54.8 us
    pallas_call x1, Pallas kernels: 59.6 us -> 54.8 us  [shards(): pl.pallas_call(functools.partial(kernel, n_tm, n_col), out_shape=(homes,...]
where the time goes in v7:
time: 57.4 us; the launch traced here: 57.3 us
  Pallas kernels  54.8 us (95%)
  other arithmetic  2.5 us (4%)
    pallas_call x1, Pallas kernels, shards(): pl.pallas_call(functools.partial(kernel, n_tm, n_col), out_shape=(homes,...  54.8 us
    add x1, other arithmetic, shards(): forward[0].astype(F32) + forward[1].astype(F32) + backward.astype(F32)  2.5 us

profile of v7, /device:TPU:29, one launch (start us, length us, event | category | flops | bytes accessed | tf_op | source)
XLA Modules:
  0.0 57.3 jit_solution(1576999875623897564)
XLA Ops:
  0.0 54.8 %shard_map.37 = (bf16[2,2,2,512,128]{4,3,2,1,0:T(8,128)(2,1)}, bf16[2,2,512,128]{3,2,1,0:T(8,128)(2,1)}) custom-call(bf16[2,2,512,128]{3,2,1,0:T(8,128)(2,1)} %near.1, bf16[2,2,512,128]{3,2,1,0:T(8,128)(2,1)} %far.1, bf16[2,2,512,128]{3,2,1,0:T(8,128)(2,1)} %meson.1), custom_call_target="tpu_custom_call" | custom-call | tf_op jit(solution)/shard_map/pallas_call | solution.py:221
  54.8 2.5 %bitcast_add_fusion = f32[2,2,512,128]{3,2,1,0:T(8,128)} fusion(bf16[2,2,512,128]{3,2,1,0:T(8,128)(2,1)} %get-tuple-element.8, bf16[2,2,2,512,128]{4,3,2,1,0:T(8,128)(2,1)} %get-tuple-element.7), kind=kLoop, calls=%fused_computation | loop fusion | flops 1310720 | bytes 2621440 | tf_op jit(solution)/shard_map/add | solution.py:235
